TPU v7x, 32 devices: a whole 2x2x4 slice. The times are simulated.
32 devices in a mesh: col: 8 (over z, x), row: 4 (over y, core).
Axes of the slice: x: 2, y: 2, z: 4, core: 2. Of those that a mesh axis runs over, the one named last changes fastest.
Arguments:
- weight: float32 [8192, 16384], P('row', 'col'), may hold values from -6 to 6
- momentum: float32 [8192, 16384], P('row', 'col'), may hold values from -6 to 6
- gradient: bfloat16 [8192, 16384], P('row', 'col'), may hold values from -6 to 6
- right_factor: float32 [16384, 256], P('col'), may hold values from -6 to 6
Outputs:
- new_weight: float32 [8192, 16384], P('row', 'col')
- new_momentum: float32 [8192, 16384], P('row', 'col')
- new_factor: float32 [16384, 256], P('col')
All inputs are finite; a program needn't handle non-finite values.
Results may differ from a plain program's by a relative error of at most 0.0003.
Values sent between devices are 32-bit elements; how exact they have to be, the bound alone decides.
No kernel may reach another device: no remote copies, remote signals or barrier semaphores. Data moves between devices by JAX's collectives and lax.ppermute only.
A program may use at most 128 MiB of HBM per device.

v0:
```python
import jax
import jax.numpy as jnp
from jax import lax
from jax.sharding import PartitionSpec as P

D_IN = 16384


def contract(first, second, first_dim, second_dim):
    return lax.dot_general(
        first,
        second,
        (((first_dim,), (second_dim,)), ((), ())),
        precision=lax.Precision.HIGHEST,
        preferred_element_type=jnp.float32,
    )


def orthonormal(left_raw, gram_matrix):
    lower = jnp.linalg.cholesky(gram_matrix)
    return lax.linalg.triangular_solve(
        lower, left_raw, left_side=False, lower=True, transpose_a=True
    )


def on_device(weight, momentum, gradient, right_factor):
    combined = momentum + gradient.astype(jnp.float32)
    partial_value = contract(combined, right_factor, 1, 0)
    left_raw = lax.psum(partial_value, "col")
    gram_matrix = lax.psum(contract(left_raw, left_raw, 0, 0), "row")
    left_factor = orthonormal(left_raw, gram_matrix)
    right_raw = lax.psum(contract(combined, left_factor, 0, 0), "row")
    squares = lax.psum(jnp.sum(right_raw * right_raw, axis=0), "col")
    new_factor = right_raw / jnp.sqrt(squares / D_IN + 1e-06)
    new_momentum = combined - 0.05 * contract(left_factor, right_raw, 1, 1)
    new_weight = weight - 0.5 * contract(left_factor, new_factor, 1, 1)
    return (new_weight, new_momentum, new_factor)


def solution(mesh):
    in_specs = (P("row", "col"), P("row", "col"), P("row", "col"), P("col", None))
    out_specs = (P("row", "col"), P("row", "col"), P("col", None))
    return jax.shard_map(
        on_device, mesh=mesh, in_specs=in_specs, out_specs=out_specs, check_vma=False
    )
```

profile of v0, /device:TPU:0, one launch (start us, length us, event | category | flops | bytes accessed | tf_op | source)
XLA Modules:
  0.0 417.1 jit_solution(15536495732991310134)
XLA Ops:
  7.2 0.0 copy-start
  7.2 0.0 all-reduce.5.cloned.1.call-start
  7.2 1.5 copy-done
  8.8 18.3 %fusion.1 = f32[2048,256]{1,0:T(8,128)} fusion(f32[2048,256]{1,0:T(8,128)S(1)} %copy-done, f32[2048,2048]{1,0:T(8,128)} %param.5, bf16[2048,2048]{1,0:T(8,128)(2,1)} %param.6), kind=kOutput, calls=%fused_computation.6 | convolution fusion | flops 12893290496 | bytes 29360128 | tf_op jit(solution)/shard_map/dot_general | solution.py:10
  27.0 0.0 all-reduce.5.cloned.1.call-update
  27.0 0.0 all-reduce.7.cloned.1.call-start
  27.1 105.1 %all-reduce.5.cloned.1.call-done = f32[2048,256]{1,0:T(8,128)} async-done(((f32[2048,256]{1,0:T(8,128)}), f32[2048,256]{1,0:T(8,128)}) %all-reduce.5.cloned.1.call-update) | async-done | bytes 2097168 | tf_op jit(solution)/shard_map/psum | solution.py:29
  132.2 6.4 %fusion.14 = f32[256,256]{0,1:T(8,128)} fusion(f32[2048,256]{1,0:T(8,128)} %all-reduce.5.cloned.1.call-done), kind=kOutput, calls=%fused_computation.40 | convolution fusion | flops 1610612736 | bytes 2359296 | tf_op jit(solution)/shard_map/dot_general | solution.py:10
  138.6 0.0 copy-start.2
  138.6 0.0 all-reduce.7.cloned.1.call-update
  138.6 0.2 all-reduce.9.cloned.1.call-start
  138.9 31.5 %all-reduce.7.cloned.1.call-done = f32[256,256]{0,1:T(8,128)} async-done(((f32[256,256]{0,1:T(8,128)}), f32[256,256]{0,1:T(8,128)}) %all-reduce.7.cloned.1.call-update) | async-done | bytes 262160 | tf_op jit(solution)/shard_map/psum | solution.py:30
  170.3 1.1 copy.8
  171.4 1.0 fusion.4
  172.4 11.7 %cholesky.50 = f32[128,128]{1,0:T(8,128)S(1)} custom-call(f32[128,128]{1,0:T(8,128)S(1)} %cholesky.118), custom_call_target="Cholesky" | custom-call | tf_op jit(solution)/shard_map/jit(cholesky)/cholesky | solution.py:20
  184.2 9.8 %custom-call.14 = f32[1,128,128]{1,2,0:T(8,128)S(1)} custom-call(f32[1,128,128]{2,1,0:T(8,128)S(1)} %get-tuple-element.24), custom_call_target="InvertDiagBlocksLowerTriangular" | custom-call | tf_op jit(solution)/shard_map/jit(cholesky)/cholesky | solution.py:20
  194.0 0.2 constant_dynamic-update-slice_fusion.1
  194.2 0.3 convolution_subtract_fusion.1
  194.5 11.7 %cholesky.105 = f32[128,128]{1,0:T(8,128)S(1)} custom-call(f32[128,128]{1,0:T(8,128)S(1)} %convolution_subtract_fusion.1), custom_call_target="Cholesky" | custom-call | tf_op jit(solution)/shard_map/jit(cholesky)/cholesky | solution.py:20
  206.3 0.6 compare_reduce_fusion
  208.2 0.1 triangular_solve.58
  208.3 4.2 %while.1 = (s32[]{:T(128)}, f32[256,256]{1,0:T(8,128)S(1)}, s32[2,2]{1,0:T(2,128)S(1)}, f32[2,128,128]{2,1,0:T(8,128)S(1)}, s32[]{:T(128)}) while((s32[]{:T(128)}, f32[256,256]{1,0:T(8,128)S(1)}, s32[2,2]{1,0:T(2,128)S(1)}, f32[2,128,128]{2,1,0:T(8,128)S(1)}, s32[]{:T(128)}) %tuple.27), condition=%wide.while_cond, body=%wide.while_body.sunk | while | flops 2 | bytes 131189 | solution.py:21
  208.5 0.6 fusion.25
  209.1 1.4 bitcast_dynamic-update-slice_fusion.2
  210.5 0.6 fusion.25
  211.1 1.4 bitcast_dynamic-update-slice_fusion.2
  212.5 19.7 %custom-call.15 = f32[2,128,128]{1,2,0:T(8,128)S(1)} custom-call(f32[2,128,128]{2,1,0:T(8,128)S(1)} %get-tuple-element.10), custom_call_target="InvertDiagBlocksLowerTriangular" | custom-call | tf_op jit(solution)/shard_map/triangular_solve | solution.py:21
  232.2 0.0 copy-done.2
  232.2 1.1 fusion.2
  233.3 1.8 convolution_subtract_fusion
  235.1 1.1 fusion.5
  236.2 0.0 copy-start.5
  236.2 32.4 %fusion = f32[2048,256]{1,0:T(8,128)} fusion(f32[2048,2048]{1,0:T(8,128)} %param.5, bf16[2048,2048]{1,0:T(8,128)(2,1)} %param.6, f32[2048,128]{0,1:T(8,128)S(1)} %fusion.5, f32[2048,128]{0,1:T(8,128)S(1)} %fusion.2), kind=kOutput, calls=%fused_computation.5 | convolution fusion | flops 12893814784 | bytes 29360128 | tf_op jit(solution)/shard_map/dot_general | solution.py:10
  268.6 0.0 copy-done.5
  268.6 0.0 all-reduce.9.cloned.1.call-update
  268.6 51.5 %all-reduce.9.cloned.1.call-done = f32[2048,256]{1,0:T(8,128)} async-done(((f32[2048,256]{1,0:T(8,128)}), f32[2048,256]{1,0:T(8,128)}) %all-reduce.9.cloned.1.call-update) | async-done | bytes 2097168 | tf_op jit(solution)/shard_map/psum | solution.py:32
  320.2 2.0 multiply_reduce_fusion
  322.2 21.3 %psum.31 = f32[256]{0:T(256)S(1)} all-reduce(f32[256]{0:T(256)S(1)} %multiply_reduce_fusion), channel_id=1, replica_groups=mesh['col'=8,'row'=4] {'col'}, use_global_device_ids=true, to_apply=%region_8.9 | all-reduce | flops 256 | bytes 2048 | tf_op jit(solution)/shard_map/psum | solution.py:33
  343.6 0.0 copy-done.3
  343.6 0.0 copy-start.6
  343.6 0.1 broadcast_divide_fusion
  343.7 0.0 copy-start.7
  343.7 1.3 copy-done.7
  345.1 0.1 copy-done.6
  345.2 31.9 %multiply_subtract_fusion.1 = f32[2048,2048]{1,0:T(8,128)} fusion(f32[2048,2048]{1,0:T(8,128)} %param.4, f32[2048,256]{1,0:T(8,128)S(1)} %broadcast_divide_fusion, f32[2048,128]{0,1:T(8,128)S(1)} %copy-done.6, f32[2048,128]{0,1:T(8,128)S(1)} %fusion.2), kind=kOutput, calls=%fused_computation.3 | convolution fusion | flops 12893814784 | bytes 37748736 | tf_op jit(solution)/shard_map/dot_general | solution.py:10
  377.1 0.0 copy-done.4
  377.1 33.3 %multiply_subtract_fusion = f32[2048,2048]{1,0:T(8,128)} fusion(f32[2048,256]{1,0:T(8,128)S(1)} %copy-done.4, f32[2048,2048]{1,0:T(8,128)} %param.5, bf16[2048,2048]{1,0:T(8,128)(2,1)} %param.6, f32[2048,128]{0,1:T(8,128)S(1)} %copy-done.6, f32[2048,128]{0,1:T(8,128)S(1)} %fusion.2), kind=kOutput, calls=%fused_computation.2 | convolution fusion | flops 12902203392 | bytes 46137344 | tf_op jit(solution)/shard_map/dot_general | solution.py:10
  410.4 0.0 copy-done.1
  (13 shorter events, 0.2 us)
Async XLA Ops:
  7.2 1.6 copy-start
  7.2 125.1 %all-reduce.5.cloned.1.call-start = ((), (), s32[]{:S(2)}) async-start(), calls=%async_computation | async-start | bytes 4194304 | tf_op jit(solution)/shard_map/psum | solution.py:29
  27.0 143.3 %all-reduce.7.cloned.1.call-start = ((), (), s32[]{:S(2)}) async-start(), calls=%async_computation.1 | async-start | bytes 524288 | tf_op jit(solution)/shard_map/psum | solution.py:30
  138.6 93.6 %copy-start.2 = (f32[2048,256]{1,0:T(8,128)S(1)}, f32[2048,256]{1,0:T(8,128)}, u32[]{:S(2)}) copy-start(f32[2048,256]{1,0:T(8,128)} %all-reduce.5.cloned.1.call-done) | copy-start | bytes 6291460
  138.6 181.5 %all-reduce.9.cloned.1.call-start = ((), (), s32[]{:S(2)}) async-start(), calls=%async_computation.2 | async-start | bytes 4194304 | tf_op jit(solution)/shard_map/psum | solution.py:32
  236.2 32.4 %copy-start.5 = (f32[2048,128]{0,1:T(8,128)}, f32[2048,128]{0,1:T(8,128)S(1)}, u32[]{:S(2)}) copy-start(f32[2048,128]{0,1:T(8,128)S(1)} %fusion.5) | copy-start | bytes 3145732
  320.2 23.4 %copy-start.3 = (f32[2048,256]{1,0:T(8,128)S(1)}, f32[2048,256]{1,0:T(8,128)}, u32[]{:S(2)}) copy-start(f32[2048,256]{1,0:T(8,128)} %all-reduce.9.cloned.1.call-done) | copy-start | bytes 6291460
  343.6 1.6 copy-start.6
  343.7 1.3 copy-start.7
  345.2 31.9 %copy-start.4 = (f32[2048,256]{1,0:T(8,128)S(1)}, f32[2048,256]{1,0:T(8,128)}, u32[]{:S(2)}) copy-start(f32[2048,256]{1,0:T(8,128)} %all-reduce.9.cloned.1.call-done) | copy-start | bytes 6291460
  377.1 33.3 %copy-start.1 = (f32[2048,256]{1,0:T(8,128)S(1)}, f32[2048,256]{1,0:T(8,128)}, u32[]{:S(2)}) copy-start(f32[2048,256]{1,0:T(8,128)} %param.7) | copy-start | bytes 6291460
Sparse Core Ops, SparseCore 0:
  27.2 105.0 all-reduce.4
  138.8 31.5 all-reduce.6
  268.8 51.3 all-reduce.8
where the time goes:
time: 424 us; the launch traced here: 417 us
  waiting for transfers between devices  188 us (44%)
  matrix products  127 us (30%)
  other arithmetic  56.8 us (13%)
  blocking collectives  21.3 us (5%)
  between operations  15.4 us (4%)
  local copies, waits for them, and re-layouts  8.11 us (2%)
    dot_general x5, matrix products, contract(): lax.dot_general(first, second, (((first_dim,), (second_dim,)), ((), ())),...  122 us
    psum x1, waiting for transfers between devices, on_device(): left_raw = lax.psum(partial_value, 'col')  105 us
    psum x1, waiting for transfers between devices, on_device(): right_raw = lax.psum(contract(combined, left_factor, 0, 0), 'row')  51.5 us
    another operation x6, other arithmetic, orthonormal(): lower = jnp.linalg.cholesky(gram_matrix)  34 us
    psum x1, waiting for transfers between devices, on_device(): gram_matrix = lax.psum(contract(left_raw, left_raw, 0, 0), 'row')  31.5 us
    psum x1, blocking collectives, on_device(): squares = lax.psum(jnp.sum(right_raw * right_raw, axis=0), 'col')  21.3 us
    another operation x3, other arithmetic, orthonormal(): lax.linalg.triangular_solve(lower, left_raw, left_side=False, lower=True,...  19.7 us
  transfers between devices with their start and end apart: 3, of which 3 were waited for; matrix products, arithmetic and copies ran while one was open for 0% of the time, Pallas kernels for 0%

commit v1 on v0

--- a/solution.py
+++ b/solution.py
@@ -4,6 +4,11 @@
 from jax.sharding import PartitionSpec as P
 
 D_IN = 16384
+
+
+def case_measure(u, group_axis):
+    z2 = jnp.sum(lax.all_gather(u, group_axis), 0)
+    return z2
 
 
 def contract(first, second, first_dim, second_dim):
@@ -26,7 +31,7 @@
 def on_device(weight, momentum, gradient, right_factor):
     combined = momentum + gradient.astype(jnp.float32)
     partial_value = contract(combined, right_factor, 1, 0)
-    left_raw = lax.psum(partial_value, "col")
+    left_raw = case_measure(partial_value, "col")
     gram_matrix = lax.psum(contract(left_raw, left_raw, 0, 0), "row")
     left_factor = orthonormal(left_raw, gram_matrix)
     right_raw = lax.psum(contract(combined, left_factor, 0, 0), "row")

time: 424 us -> 562 us (1.33)
  waiting for transfers between devices: 188 us -> 312 us
  other arithmetic: 56.8 us -> 64 us
  matrix products: 127 us -> 133 us
    all_gather x0 -> x1, waiting for transfers between devices: none -> 230 us  [case_measure(): z2 = jnp.sum(lax.all_gather(u, group_axis), 0)]
    psum x1 -> x0, waiting for transfers between devices: 105 us -> none  [on_device(): left_raw = lax.psum(partial_value, 'col')]
    reduce_sum x0 -> x1, other arithmetic: none -> 7.14 us  [case_measure(): z2 = jnp.sum(lax.all_gather(u, group_axis), 0)]
    dot_general x5, matrix products: 122 us -> 129 us  [contract(): lax.dot_general(first, second, (((first_dim,), (second_dim,)), ((), ())),...]
where the time goes in v1:
time: 562 us; the launch traced here: 555 us
  waiting for transfers between devices  312 us (56%)
  matrix products  133 us (24%)
  other arithmetic  64 us (11%)
  blocking collectives  21.3 us (4%)
  between operations  15.7 us (3%)
  local copies, waits for them, and re-layouts  8.11 us (1%)
    all_gather x1, waiting for transfers between devices, case_measure(): z2 = jnp.sum(lax.all_gather(u, group_axis), 0)  230 us
    dot_general x5, matrix products, contract(): lax.dot_general(first, second, (((first_dim,), (second_dim,)), ((), ())),...  129 us
    psum x1, waiting for transfers between devices, on_device(): right_raw = lax.psum(contract(combined, left_factor, 0, 0), 'row')  51.5 us
    another operation x6, other arithmetic, orthonormal(): lower = jnp.linalg.cholesky(gram_matrix)  33.9 us
    psum x1, waiting for transfers between devices, on_device(): gram_matrix = lax.psum(contract(left_raw, left_raw, 0, 0), 'row')  30.3 us
    psum x1, blocking collectives, on_device(): squares = lax.psum(jnp.sum(right_raw * right_raw, axis=0), 'col')  21.3 us
    another operation x3, other arithmetic, orthonormal(): lax.linalg.triangular_solve(lower, left_raw, left_side=False, lower=True,...  19.7 us
  transfers between devices with their start and end apart: 3, of which 3 were waited for; matrix products, arithmetic and copies ran while one was open for 0% of the time, Pallas kernels for 0%

profile of v1, /device:TPU:0, one launch (start us, length us, event | category | flops | bytes accessed | tf_op | source)
XLA Modules:
  0.0 554.7 jit_solution(12251417694212683297)
XLA Ops:
  7.2 0.0 copy-start
  7.2 0.0 all-gather.3.cloned.1.call-start
  7.2 1.5 copy-done
  8.8 18.2 %fusion.1 = f32[2048,256]{1,0:T(8,128)} fusion(f32[2048,256]{1,0:T(8,128)S(1)} %copy-done, f32[2048,2048]{1,0:T(8,128)} %param.5, bf16[2048,2048]{1,0:T(8,128)(2,1)} %param.6), kind=kOutput, calls=%fused_computation.6 | convolution fusion | flops 12893290496 | bytes 29360128 | tf_op jit(solution)/shard_map/dot_general | solution.py:15
  27.0 0.0 all-gather.3.cloned.1.call-update
  27.0 0.0 all-reduce.4.cloned.1.call-start
  27.1 230.1 %all-gather.3.cloned.1.call-done = f32[16384,256]{1,0:T(8,128)} async-done(((f32[2048,256]{1,0:T(8,128)}), f32[16384,256]{1,0:T(8,128)}) %all-gather.3.cloned.1.call-update) | async-done | bytes 16777232 | tf_op jit(solution)/shard_map/all_gather | solution.py:10
  257.2 7.1 %reduce_sum.18 = f32[2048,256]{1,0:T(8,128)S(1)} reduce(f32[8,2048,256]{2,1,0:T(8,128)} %bitcast.37, f32[]{:T(128)} %constant.77.clone.1), dimensions={0}, to_apply=%region_0.0 | reduce | flops 3670016 | bytes 18874372 | tf_op jit(solution)/shard_map/reduce_sum | solution.py:10
  264.3 4.2 fusion.14
  268.5 0.0 all-reduce.4.cloned.1.call-update
  268.5 0.3 all-reduce.6.cloned.1.call-start
  268.9 30.3 %all-reduce.4.cloned.1.call-done = f32[256,256]{0,1:T(8,128)} async-done(((f32[256,256]{0,1:T(8,128)}), f32[256,256]{0,1:T(8,128)}) %all-reduce.4.cloned.1.call-update) | async-done | bytes 262160 | tf_op jit(solution)/shard_map/psum | solution.py:35
  299.2 1.1 copy.8
  300.2 1.0 fusion.4
  301.2 11.7 %cholesky.50 = f32[128,128]{1,0:T(8,128)S(1)} custom-call(f32[128,128]{1,0:T(8,128)S(1)} %cholesky.118), custom_call_target="Cholesky" | custom-call | tf_op jit(solution)/shard_map/jit(cholesky)/cholesky | solution.py:25
  313.0 9.8 %custom-call.14 = f32[1,128,128]{1,2,0:T(8,128)S(1)} custom-call(f32[1,128,128]{2,1,0:T(8,128)S(1)} %get-tuple-element.24), custom_call_target="InvertDiagBlocksLowerTriangular" | custom-call | tf_op jit(solution)/shard_map/jit(cholesky)/cholesky | solution.py:25
  322.8 0.2 constant_dynamic-update-slice_fusion.1
  323.0 0.3 convolution_subtract_fusion.1
  323.3 11.7 %cholesky.105 = f32[128,128]{1,0:T(8,128)S(1)} custom-call(f32[128,128]{1,0:T(8,128)S(1)} %convolution_subtract_fusion.1), custom_call_target="Cholesky" | custom-call | tf_op jit(solution)/shard_map/jit(cholesky)/cholesky | solution.py:25
  335.1 0.6 compare_reduce_fusion
  337.0 0.1 triangular_solve.58
  337.1 4.0 while.1
  337.1 0.6 fusion.25
  337.7 1.4 bitcast_dynamic-update-slice_fusion.2
  339.1 0.6 fusion.25
  339.7 1.4 bitcast_dynamic-update-slice_fusion.2
  341.1 19.7 %custom-call.15 = f32[2,128,128]{1,2,0:T(8,128)S(1)} custom-call(f32[2,128,128]{2,1,0:T(8,128)S(1)} %get-tuple-element.10), custom_call_target="InvertDiagBlocksLowerTriangular" | custom-call | tf_op jit(solution)/shard_map/triangular_solve | solution.py:26
  360.8 1.1 fusion.2
  361.9 1.8 convolution_subtract_fusion
  363.7 1.1 fusion.5
  364.8 0.0 copy-start.4
  364.8 41.1 %fusion = f32[2048,256]{1,0:T(8,128)} fusion(f32[2048,2048]{1,0:T(8,128)} %param.5, bf16[2048,2048]{1,0:T(8,128)(2,1)} %param.6, f32[2048,128]{0,1:T(8,128)S(1)} %fusion.5, f32[2048,128]{0,1:T(8,128)S(1)} %fusion.2), kind=kOutput, calls=%fused_computation.5 | convolution fusion | flops 12893814784 | bytes 29360128 | tf_op jit(solution)/shard_map/dot_general | solution.py:15
  405.9 0.0 copy-done.4
  405.9 0.0 all-reduce.6.cloned.1.call-update
  406.0 51.5 %all-reduce.6.cloned.1.call-done = f32[2048,256]{1,0:T(8,128)} async-done(((f32[2048,256]{1,0:T(8,128)}), f32[2048,256]{1,0:T(8,128)}) %all-reduce.6.cloned.1.call-update) | async-done | bytes 2097168 | tf_op jit(solution)/shard_map/psum | solution.py:37
  457.5 0.0 copy-start.2
  457.5 2.0 multiply_reduce_fusion
  459.5 21.3 %psum.23 = f32[256]{0:T(256)S(1)} all-reduce(f32[256]{0:T(256)S(1)} %multiply_reduce_fusion), channel_id=1, replica_groups=mesh['col'=8,'row'=4] {'col'}, use_global_device_ids=true, to_apply=%region_8.9 | all-reduce | flops 256 | bytes 2048 | tf_op jit(solution)/shard_map/psum | solution.py:38
  480.9 0.0 copy-done.2
  480.9 0.0 copy-start.5
  480.9 0.1 broadcast_divide_fusion
  481.0 0.0 copy-start.6
  481.1 1.3 copy-done.6
  482.4 0.1 copy-done.5
  482.5 31.9 %multiply_subtract_fusion.1 = f32[2048,2048]{1,0:T(8,128)} fusion(f32[2048,2048]{1,0:T(8,128)} %param.4, f32[2048,256]{1,0:T(8,128)S(1)} %broadcast_divide_fusion, f32[2048,128]{0,1:T(8,128)S(1)} %copy-done.5, f32[2048,128]{0,1:T(8,128)S(1)} %fusion.2), kind=kOutput, calls=%fused_computation.3 | convolution fusion | flops 12893814784 | bytes 37748736 | tf_op jit(solution)/shard_map/dot_general | solution.py:15
  514.4 0.0 copy-done.3
  514.4 33.4 %multiply_subtract_fusion = f32[2048,2048]{1,0:T(8,128)} fusion(f32[2048,256]{1,0:T(8,128)S(1)} %copy-done.3, f32[2048,2048]{1,0:T(8,128)} %param.5, bf16[2048,2048]{1,0:T(8,128)(2,1)} %param.6, f32[2048,128]{0,1:T(8,128)S(1)} %copy-done.5, f32[2048,128]{0,1:T(8,128)S(1)} %fusion.2), kind=kOutput, calls=%fused_computation.2 | convolution fusion | flops 12902203392 | bytes 46137344 | tf_op jit(solution)/shard_map/dot_general | solution.py:15
  547.8 0.0 copy-done.1
  (12 shorter events, 0.2 us)
Async XLA Ops:
  7.2 1.6 copy-start
  7.2 250.0 %all-gather.3.cloned.1.call-start = ((), (), s32[]{:S(2)}) async-start(), calls=%async_computation.2 | async-start | bytes 18874368 | tf_op jit(solution)/shard_map/all_gather | solution.py:10
  27.0 272.1 %all-reduce.4.cloned.1.call-start = ((), (), s32[]{:S(2)}) async-start(), calls=%async_computation | async-start | bytes 524288 | tf_op jit(solution)/shard_map/psum | solution.py:35
  268.5 189.0 %all-reduce.6.cloned.1.call-start = ((), (), s32[]{:S(2)}) async-start(), calls=%async_computation.1 | async-start | bytes 4194304 | tf_op jit(solution)/shard_map/psum | solution.py:37
  364.8 41.1 %copy-start.4 = (f32[2048,128]{0,1:T(8,128)}, f32[2048,128]{0,1:T(8,128)S(1)}, u32[]{:S(2)}) copy-start(f32[2048,128]{0,1:T(8,128)S(1)} %fusion.5) | copy-start | bytes 3145732
  457.5 23.4 %copy-start.2 = (f32[2048,256]{1,0:T(8,128)S(1)}, f32[2048,256]{1,0:T(8,128)}, u32[]{:S(2)}) copy-start(f32[2048,256]{1,0:T(8,128)} %all-reduce.6.cloned.1.call-done) | copy-start | bytes 6291460
  480.9 1.6 copy-start.5
  481.0 1.3 copy-start.6
  482.5 31.9 %copy-start.3 = (f32[2048,256]{1,0:T(8,128)S(1)}, f32[2048,256]{1,0:T(8,128)}, u32[]{:S(2)}) copy-start(f32[2048,256]{1,0:T(8,128)} %all-reduce.6.cloned.1.call-done) | copy-start | bytes 6291460
  514.4 33.4 %copy-start.1 = (f32[2048,256]{1,0:T(8,128)S(1)}, f32[2048,256]{1,0:T(8,128)}, u32[]{:S(2)}) copy-start(f32[2048,256]{1,0:T(8,128)} %param.7) | copy-start | bytes 6291460
Sparse Core Ops, SparseCore 0:
  27.2 229.9 all-gather.2
  268.6 30.4 all-reduce.3
  406.1 51.3 all-reduce.5
